TPU v7x, 128 devices: a whole 4x4x4 slice. The times are simulated.
128 devices in a mesh: sample: 8 (over y_hi, z), landmark: 16 (over y_lo, x, core).
Axes of the slice: x: 4, y: 4 (y_hi: 2, y_lo: 2; y = y_hi * 2 + y_lo), z: 4, core: 2. Of those that a mesh axis runs over, the one named last changes fastest.
Arguments:
- embeddings: bfloat16 [8192, 4096], P('sample'), may hold values from -6 to 6
- landmarks: bfloat16 [16384, 4096], P('landmark'), may hold values from -6 to 6
- factor: bfloat16 [16384, 16384], P('landmark', 'sample')
- flips: int32 [512, 8192], P(None, 'sample'), may hold values from 0 to 1
- labels: int32 [8192], P('sample'), may hold values from 0 to 1, as said below
- counts: int32 [8], replicated, may hold values from 256 to 1024, as said below
Outputs:
- whitened: bfloat16 [16384, 512], P(('sample', 'landmark'))
- statistic: float32 [512], replicated
Inputs may be any that keep to these rules, and one draw needn't show every extreme that they name: `counts`: one slab holds exactly 1024 live rows. `labels`: 0 or 1; the first slot of every slab is of corpus 0 and the second of corpus 1.
All inputs are finite; a program needn't handle non-finite values.
Results may differ from a plain program's by a relative error of at most 0.029.
Values may be sent and summed in bfloat16 or wider, within the bound.
A program may use at most 128 MiB of HBM per device.

v0:
```python
import math
import jax
import jax.numpy as jnp
from jax import lax
from jax.sharding import PartitionSpec as P

D = 4096
LANDMARKS = 16384


def whiten_maker(factor, moments_half):
    return lax.dot_general(
        factor, moments_half, (((0,), (1,)), ((), ())), preferred_element_type=jnp.float32
    )


def local(embeddings, landmarks, factor, flips, labels, counts):
    slot_count = embeddings.shape[0]
    slab_total = counts.shape[0]
    here_index = lax.axis_index("sample")
    own_count = jnp.sum(jnp.where(jnp.arange(slab_total, dtype=jnp.int32) == here_index, counts, 0))
    live_rows = (jnp.arange(slot_count, dtype=jnp.int32) < own_count).astype(jnp.float32)
    corpus = labels.astype(jnp.float32)
    count_a, count_b = lax.psum(
        (jnp.sum(live_rows * (1.0 - corpus)), jnp.sum(live_rows * corpus)), "sample"
    )
    balance = jnp.sqrt(count_a * count_b / (count_a + count_b))
    row_weight = live_rows * ((1.0 - corpus) / count_a - corpus / count_b) * balance
    wide_x = embeddings.astype(jnp.float32)
    row_scale = lax.rsqrt(jnp.mean(wide_x * wide_x, axis=1) + 1e-06)
    wide_z = landmarks.astype(jnp.float32)
    point_scale = lax.rsqrt(jnp.mean(wide_z * wide_z, axis=1) + 1e-06)
    signs = (2 * flips - 1).astype(jnp.bfloat16)
    cross = lax.dot_general(
        embeddings, landmarks, (((1,), (1,)), ((), ())), preferred_element_type=jnp.float32
    )
    kern = jnp.exp(0.5 * cross * row_scale[:, None] * point_scale[None, :] / math.sqrt(D))
    weighted = (row_weight[:, None] * kern).astype(jnp.bfloat16)
    partial_value = jnp.dot(signs, weighted, preferred_element_type=jnp.float32)
    summed = lax.psum(partial_value.astype(jnp.bfloat16), "sample")
    wide = lax.psum_scatter(
        whiten_maker(factor, summed).astype(jnp.bfloat16),
        "landmark",
        scatter_dimension=0,
        tiled=True,
    ).astype(jnp.float32)
    share = jnp.sum(wide * wide, axis=0)
    statistic = lax.psum(share, ("sample", "landmark")) / LANDMARKS
    return (wide.astype(jnp.bfloat16), statistic)


def solution(mesh):
    return jax.shard_map(
        local,
        mesh=mesh,
        in_specs=(
            P("sample", None),
            P("landmark", None),
            P("landmark", "sample"),
            P(None, "sample"),
            P("sample"),
            P(),
        ),
        out_specs=(P(("sample", "landmark"), None), P()),
        check_vma=False,
    )
```

profile of v0, /device:TPU:1, one launch (start us, length us, event | category | flops | bytes accessed | tf_op | source)
XLA Modules:
  0.0 293.1 jit_solution(10554155324927165992)
XLA Ops:
  7.2 0.0 all-reduce.3.cloned.1.call-start
  7.2 1.3 fusion.9
  8.5 2.0 select_reduce_fusion
  10.5 23.3 %all-reduce = (f32[]{:T(128)}, f32[]{:T(128)}) all-reduce(f32[]{:T(128)} %get-tuple-element.7, f32[]{:T(128)} %get-tuple-element.6), channel_id=1, replica_groups=mesh['sample'=8,'landmark'=16] {'sample'}, use_global_device_ids=true, to_apply=%region_2.3 | all-reduce | flops 2 | bytes 16 | tf_op jit(solution)/shard_map/psum | solution.py:24
  36.3 2.5 select_multiply_fusion
  38.9 0.0 copy-start
  38.9 5.2 %multiply_reduce_fusion.1 = f32[1024]{0:T(1024)S(1)} fusion(bf16[1024,4096]{1,0:T(8,128)(2,1)} %param.6), kind=kLoop, calls=%fused_computation.1 | loop fusion | flops 12581888 | bytes 8392704 | tf_op jit(solution)/shard_map/reduce_sum | solution.py:30
  44.1 0.5 copy-done
  44.7 0.0 copy-start.1
  44.7 1.7 multiply_reduce_fusion
  46.4 0.0 copy-done.1
  46.4 16.2 %fusion.6 = bf16[512,1024]{1,0:T(8,128)(2,1)} fusion(bf16[1024,4096]{1,0:T(8,128)(2,1)} %param.6, bf16[1024,4096]{1,0:T(8,128)(2,1)} %param.7, f32[1024]{0:T(1024)S(1)} %get-tuple-element.10, f32[1024]{0:T(1024)S(1)} %get-tuple-element.11, f32[1024]{0:T(1024)S(1)} %select_multiply_fusion, s32[512,1024]{1,0:T(8,128)S(1)} %copy-done.1), kind=kOutput, calls=%fused_computation.11 | convolution fusion | flops 9671016448 | bytes 19935232 | tf_op jit(solution)/shard_map/dot_general | solution.py:39
  62.6 0.0 all-reduce.3.cloned.1.call-update
  62.6 0.0 reduce-scatter.4.cloned.1.call-start
  62.7 83.6 %all-reduce.3.cloned.1.call-done = bf16[512,1024]{1,0:T(8,128)(2,1)} async-done(((bf16[512,1024]{1,0:T(8,128)(2,1)}), bf16[512,1024]{1,0:T(8,128)(2,1)}) %all-reduce.3.cloned.1.call-update) | async-done | bytes 1048592 | tf_op jit(solution)/shard_map/psum | solution.py:40
  146.3 4.8 %fusion = bf16[2048,512]{0,1:T(8,128)(2,1)S(1)} fusion(bf16[512,1024]{1,0:T(8,128)(2,1)} %all-reduce.3.cloned.1.call-done, bf16[1024,2048]{1,0:T(8,128)(2,1)} %param.8), kind=kOutput, calls=%fused_computation.4 | convolution fusion | flops 2148532224 | bytes 7340032 | tf_op jit(solution)/shard_map/dot_general | solution.py:12
  151.1 2.5 copy.10
  153.6 0.0 reduce-scatter.4.cloned.1.call-update
  153.7 62.8 %reduce-scatter.4.cloned.1.call-done = bf16[128,512]{1,0:T(8,128)(2,1)} async-done(((bf16[2048,512]{1,0:T(8,128)(2,1)}), bf16[128,512]{1,0:T(8,128)(2,1)}) %reduce-scatter.4.cloned.1.call-update) | async-done | bytes 131088
  216.4 1.0 copy.11
  217.4 0.2 multiply_reduce_fusion.2
  217.6 68.1 %psum.31 = f32[512]{0:T(512)S(1)} all-reduce(f32[512]{0:T(512)S(1)} %multiply_reduce_fusion.2), channel_id=1, replica_groups=mesh['sample'=8,'landmark'=16] {'sample','landmark'}, use_global_device_ids=true, to_apply=%region_10.11 | all-reduce | flops 512 | bytes 4096 | tf_op jit(solution)/shard_map/psum | solution.py:48
  285.7 0.6 broadcast_multiply_fusion
  (1 shorter events, 0.0 us)
Async XLA Ops:
  7.2 139.1 %all-reduce.3.cloned.1.call-start = ((), (), s32[]{:S(2)}) async-start(), calls=%async_computation.1 | async-start | bytes 2097152 | tf_op jit(solution)/shard_map/psum | solution.py:40
  38.9 5.8 %copy-start = (bf16[1024,4096]{1,0:T(8,128)(2,1)S(1)}, bf16[1024,4096]{1,0:T(8,128)(2,1)}, u32[]{:S(2)}) copy-start(bf16[1024,4096]{1,0:T(8,128)(2,1)} %param.7) | copy-start | bytes 25165828
  44.7 1.7 copy-start.1
  62.6 153.8 %reduce-scatter.4.cloned.1.call-start = ((), (), s32[]{:S(2)}) async-start(), calls=%async_computation.2 | async-start | bytes 2228224
Sparse Core Ops, SparseCore 0:
  62.7 83.4 all-reduce.2
  153.8 62.5 reduce-scatter.3
where the time goes:
time: 293 us
  waiting for transfers between devices  146 us (50%)
  blocking collectives  91.4 us (31%)
  matrix products  21.1 us (7%)
  between operations  16.6 us (6%)
  other arithmetic  13.5 us (5%)
  local copies, waits for them, and re-layouts  4.09 us (1%)
    psum x1, waiting for transfers between devices, local(): summed = lax.psum(partial_value.astype(jnp.bfloat16), 'sample')  83.6 us
    psum x1, blocking collectives, local(): statistic = lax.psum(share, ('sample', 'landmark')) / LANDMARKS  68.1 us
    unnamed x3, waiting for transfers between devices  62.8 us
    psum x1, blocking collectives, local(): lax.psum((jnp.sum(live_rows * (1.0 - corpus)), jnp.sum(live_rows * corpus...  23.3 us
    dot_general x1, matrix products, local(): partial_value = jnp.dot(signs, weighted, preferred_element_type=jnp.float32)  16.2 us
  transfers between devices with their start and end apart: 2, of which 2 were waited for; matrix products, arithmetic and copies ran while one was open for 0% of the time, Pallas kernels for 0%

commit v1 on v0

--- a/solution.py
+++ b/solution.py
@@ -37,7 +37,7 @@
     kern = jnp.exp(0.5 * cross * row_scale[:, None] * point_scale[None, :] / math.sqrt(D))
     weighted = (row_weight[:, None] * kern).astype(jnp.bfloat16)
     partial_value = jnp.dot(signs, weighted, preferred_element_type=jnp.float32)
-    summed = lax.psum(partial_value.astype(jnp.bfloat16), "sample")
+    summed = jnp.sum(lax.all_gather(partial_value.astype(jnp.bfloat16), "sample"), axis=0)
     wide = lax.psum_scatter(
         whiten_maker(factor, summed).astype(jnp.bfloat16),
         "landmark",

time: 293 us -> 318 us (1.085)
  waiting for transfers between devices: 146 us -> 165 us
  other arithmetic: 13.5 us -> 19.2 us
    all_gather x0 -> x1, waiting for transfers between devices: none -> 107 us  [local(): lax.all_gather(partial_value.astype(jnp.bfloat16), 'sample')]
    psum x1 -> x0, waiting for transfers between devices: 83.6 us -> none  [local(): summed = lax.psum(partial_value.astype(jnp.bfloat16), 'sample')]
    reduce_sum x0 -> x1, other arithmetic: none -> 5.66 us  [local(): jnp.sum(lax.all_gather(partial_value.astype(jnp.bfloat16), 'sample'), axi...]
    unnamed x3, waiting for transfers between devices: 62.8 us -> 57.8 us
where the time goes in v1:
time: 318 us
  waiting for transfers between devices  165 us (52%)
  blocking collectives  91.7 us (29%)
  matrix products  20.7 us (7%)
  other arithmetic  19.2 us (6%)
  between operations  16.6 us (5%)
  local copies, waits for them, and re-layouts  4.09 us (1%)
    all_gather x1, waiting for transfers between devices, local(): lax.all_gather(partial_value.astype(jnp.bfloat16), 'sample')  107 us
    psum x1, blocking collectives, local(): statistic = lax.psum(share, ('sample', 'landmark')) / LANDMARKS  68.4 us
    unnamed x3, waiting for transfers between devices  57.8 us
    psum x1, blocking collectives, local(): lax.psum((jnp.sum(live_rows * (1.0 - corpus)), jnp.sum(live_rows * corpus...  23.3 us
    dot_general x1, matrix products, local(): partial_value = jnp.dot(signs, weighted, preferred_element_type=jnp.float32)  16.2 us
  transfers between devices with their start and end apart: 2, of which 2 were waited for; matrix products, arithmetic and copies ran while one was open for 0% of the time, Pallas kernels for 0%

profile of v1, /device:TPU:1, one launch (start us, length us, event | category | flops | bytes accessed | tf_op | source)
XLA Modules:
  0.0 317.7 jit_solution(42927059822604455)
XLA Ops:
  7.2 0.0 all-gather.3.cloned.1.call-start
  7.2 1.3 fusion.9
  8.5 2.0 select_reduce_fusion
  10.5 23.3 %all-reduce = (f32[]{:T(128)}, f32[]{:T(128)}) all-reduce(f32[]{:T(128)} %get-tuple-element.7, f32[]{:T(128)} %get-tuple-element.6), channel_id=1, replica_groups=mesh['sample'=8,'landmark'=16] {'sample'}, use_global_device_ids=true, to_apply=%region_2.3 | all-reduce | flops 2 | bytes 16 | tf_op jit(solution)/shard_map/psum | solution.py:24
  36.3 2.5 select_multiply_fusion
  38.9 0.0 copy-start
  38.9 5.2 %multiply_reduce_fusion.1 = f32[1024]{0:T(1024)S(1)} fusion(bf16[1024,4096]{1,0:T(8,128)(2,1)} %param.6), kind=kLoop, calls=%fused_computation.1 | loop fusion | flops 12581888 | bytes 8392704 | tf_op jit(solution)/shard_map/reduce_sum | solution.py:30
  44.1 0.5 copy-done
  44.7 0.0 copy-start.1
  44.7 1.7 multiply_reduce_fusion
  46.4 0.0 copy-done.1
  46.4 16.2 %fusion.6 = bf16[512,1024]{1,0:T(8,128)(2,1)} fusion(bf16[1024,4096]{1,0:T(8,128)(2,1)} %param.6, bf16[1024,4096]{1,0:T(8,128)(2,1)} %param.7, f32[1024]{0:T(1024)S(1)} %get-tuple-element.10, f32[1024]{0:T(1024)S(1)} %get-tuple-element.11, f32[1024]{0:T(1024)S(1)} %select_multiply_fusion, s32[512,1024]{1,0:T(8,128)S(1)} %copy-done.1), kind=kOutput, calls=%fused_computation.11 | convolution fusion | flops 9671016448 | bytes 19935232 | tf_op jit(solution)/shard_map/dot_general | solution.py:39
  62.6 0.0 all-gather.3.cloned.1.call-update
  62.6 0.2 reduce-scatter.4.cloned.1.call-start
  62.8 107.3 %all-gather.3.cloned.1.call-done = bf16[4096,1024]{1,0:T(8,128)(2,1)} async-done(((bf16[512,1024]{1,0:T(8,128)(2,1)}), bf16[4096,1024]{1,0:T(8,128)(2,1)}) %all-gather.3.cloned.1.call-update) | async-done | bytes 8388624 | tf_op jit(solution)/shard_map/all_gather | solution.py:40
  170.1 5.7 %reduce_sum.71 = bf16[512,1024]{1,0:T(8,128)(2,1)S(1)} reduce(bf16[8,512,1024]{2,1,0:T(8,128)(2,1)} %bitcast.8, bf16[]{:T(256)} %constant.34.clone.1), dimensions={0}, to_apply=%region_7.8 | reduce | flops 3670016 | bytes 9437186 | tf_op jit(solution)/shard_map/reduce_sum | solution.py:40
  175.8 4.5 %fusion = bf16[2048,512]{0,1:T(8,128)(2,1)S(1)} fusion(bf16[512,1024]{1,0:T(8,128)(2,1)S(1)} %reduce_sum.71, bf16[1024,2048]{1,0:T(8,128)(2,1)} %param.8), kind=kOutput, calls=%fused_computation.4 | convolution fusion | flops 2148532224 | bytes 7340032 | tf_op jit(solution)/shard_map/dot_general | solution.py:12
  180.3 2.5 copy.10
  182.9 0.0 reduce-scatter.4.cloned.1.call-update
  182.9 57.8 %reduce-scatter.4.cloned.1.call-done = bf16[128,512]{1,0:T(8,128)(2,1)} async-done(((bf16[2048,512]{1,0:T(8,128)(2,1)}), bf16[128,512]{1,0:T(8,128)(2,1)}) %reduce-scatter.4.cloned.1.call-update) | async-done | bytes 131088
  240.7 1.0 copy.11
  241.7 0.2 multiply_reduce_fusion.2
  241.8 68.4 %psum.23 = f32[512]{0:T(512)S(1)} all-reduce(f32[512]{0:T(512)S(1)} %multiply_reduce_fusion.2), channel_id=1, replica_groups=mesh['sample'=8,'landmark'=16] {'sample','landmark'}, use_global_device_ids=true, to_apply=%region_10.11 | all-reduce | flops 512 | bytes 4096 | tf_op jit(solution)/shard_map/psum | solution.py:48
  310.2 0.6 broadcast_multiply_fusion
  (1 shorter events, 0.0 us)
Async XLA Ops:
  7.2 163.0 %all-gather.3.cloned.1.call-start = ((), (), s32[]{:S(2)}) async-start(), calls=%async_computation.1 | async-start | bytes 9437184 | tf_op jit(solution)/shard_map/all_gather | solution.py:40
  38.9 5.8 %copy-start = (bf16[1024,4096]{1,0:T(8,128)(2,1)S(1)}, bf16[1024,4096]{1,0:T(8,128)(2,1)}, u32[]{:S(2)}) copy-start(bf16[1024,4096]{1,0:T(8,128)(2,1)} %param.7) | copy-start | bytes 25165828
  44.7 1.7 copy-start.1
  62.6 178.1 %reduce-scatter.4.cloned.1.call-start = ((), (), s32[]{:S(2)}) async-start(), calls=%async_computation.2 | async-start | bytes 2228224
Sparse Core Ops, SparseCore 0:
  62.7 107.3 all-gather.2
  183.0 57.5 reduce-scatter.3

commit v2 on v0

--- a/solution.py
+++ b/solution.py
@@ -45,7 +45,7 @@
         tiled=True,
     ).astype(jnp.float32)
     share = jnp.sum(wide * wide, axis=0)
-    statistic = lax.psum(share, ("sample", "landmark")) / LANDMARKS
+    statistic = lax.psum(lax.psum(share, "sample"), "landmark") / LANDMARKS
     return (wide.astype(jnp.bfloat16), statistic)
 
 

time: 293 us -> 280 us (0.956)
  blocking collectives: 91.4 us -> 78.2 us
    psum x1 -> x2, blocking collectives: 68.1 us -> 54.9 us  [local(): statistic = lax.psum(lax.psum(share, 'sample'), 'landmark') / LANDMARKS]
where the time goes in v2:
time: 280 us
  waiting for transfers between devices  146 us (52%)
  blocking collectives  78.2 us (28%)
  matrix products  21.1 us (8%)
  between operations  16.6 us (6%)
  other arithmetic  13.5 us (5%)
  local copies, waits for them, and re-layouts  4.09 us (1%)
    psum x1, waiting for transfers between devices, local(): summed = lax.psum(partial_value.astype(jnp.bfloat16), 'sample')  83.6 us
    unnamed x3, waiting for transfers between devices  62.8 us
    psum x2, blocking collectives, local(): statistic = lax.psum(lax.psum(share, 'sample'), 'landmark') / LANDMARKS  54.9 us
    psum x1, blocking collectives, local(): lax.psum((jnp.sum(live_rows * (1.0 - corpus)), jnp.sum(live_rows * corpus...  23.3 us
    dot_general x1, matrix products, local(): partial_value = jnp.dot(signs, weighted, preferred_element_type=jnp.float32)  16.2 us
  transfers between devices with their start and end apart: 2, of which 2 were waited for; matrix products, arithmetic and copies ran while one was open for 0% of the time, Pallas kernels for 0%

profile of v2, /device:TPU:1, one launch (start us, length us, event | category | flops | bytes accessed | tf_op | source)
XLA Modules:
  0.0 279.9 jit_solution(16586349000923222312)
XLA Ops:
  7.2 0.0 all-reduce.3.cloned.1.call-start
  7.2 1.3 fusion.9
  8.5 2.0 select_reduce_fusion
  10.5 23.3 %all-reduce = (f32[]{:T(128)}, f32[]{:T(128)}) all-reduce(f32[]{:T(128)} %get-tuple-element.7, f32[]{:T(128)} %get-tuple-element.6), channel_id=1, replica_groups=mesh['sample'=8,'landmark'=16] {'sample'}, use_global_device_ids=true, to_apply=%region_2.3 | all-reduce | flops 2 | bytes 16 | tf_op jit(solution)/shard_map/psum | solution.py:24
  36.3 2.5 select_multiply_fusion
  38.9 0.0 copy-start
  38.9 5.2 %multiply_reduce_fusion.1 = f32[1024]{0:T(1024)S(1)} fusion(bf16[1024,4096]{1,0:T(8,128)(2,1)} %param.6), kind=kLoop, calls=%fused_computation.1 | loop fusion | flops 12581888 | bytes 8392704 | tf_op jit(solution)/shard_map/reduce_sum | solution.py:30
  44.1 0.5 copy-done
  44.7 0.0 copy-start.1
  44.7 1.7 multiply_reduce_fusion
  46.4 0.0 copy-done.1
  46.4 16.2 %fusion.6 = bf16[512,1024]{1,0:T(8,128)(2,1)} fusion(bf16[1024,4096]{1,0:T(8,128)(2,1)} %param.6, bf16[1024,4096]{1,0:T(8,128)(2,1)} %param.7, f32[1024]{0:T(1024)S(1)} %get-tuple-element.10, f32[1024]{0:T(1024)S(1)} %get-tuple-element.11, f32[1024]{0:T(1024)S(1)} %select_multiply_fusion, s32[512,1024]{1,0:T(8,128)S(1)} %copy-done.1), kind=kOutput, calls=%fused_computation.11 | convolution fusion | flops 9671016448 | bytes 19935232 | tf_op jit(solution)/shard_map/dot_general | solution.py:39
  62.6 0.0 all-reduce.3.cloned.1.call-update
  62.6 0.0 reduce-scatter.4.cloned.1.call-start
  62.7 83.6 %all-reduce.3.cloned.1.call-done = bf16[512,1024]{1,0:T(8,128)(2,1)} async-done(((bf16[512,1024]{1,0:T(8,128)(2,1)}), bf16[512,1024]{1,0:T(8,128)(2,1)}) %all-reduce.3.cloned.1.call-update) | async-done | bytes 1048592 | tf_op jit(solution)/shard_map/psum | solution.py:40
  146.3 4.8 %fusion = bf16[2048,512]{0,1:T(8,128)(2,1)S(1)} fusion(bf16[512,1024]{1,0:T(8,128)(2,1)} %all-reduce.3.cloned.1.call-done, bf16[1024,2048]{1,0:T(8,128)(2,1)} %param.8), kind=kOutput, calls=%fused_computation.4 | convolution fusion | flops 2148532224 | bytes 7340032 | tf_op jit(solution)/shard_map/dot_general | solution.py:12
  151.1 2.5 copy.10
  153.6 0.0 reduce-scatter.4.cloned.1.call-update
  153.7 62.8 %reduce-scatter.4.cloned.1.call-done = bf16[128,512]{1,0:T(8,128)(2,1)} async-done(((bf16[2048,512]{1,0:T(8,128)(2,1)}), bf16[128,512]{1,0:T(8,128)(2,1)}) %reduce-scatter.4.cloned.1.call-update) | async-done | bytes 131088
  216.4 1.0 copy.11
  217.4 0.2 multiply_reduce_fusion.2
  217.6 20.7 %psum.38 = f32[512]{0:T(512)S(1)} all-reduce(f32[512]{0:T(512)S(1)} %multiply_reduce_fusion.2), channel_id=1, replica_groups=mesh['sample'=8,'landmark'=16] {'sample'}, use_global_device_ids=true, to_apply=%region_10.11 | all-reduce | flops 512 | bytes 4096 | tf_op jit(solution)/shard_map/psum | solution.py:48
  238.3 34.2 %psum.39 = f32[512]{0:T(512)S(1)} all-reduce(f32[512]{0:T(512)S(1)} %psum.38), channel_id=1, replica_groups=mesh['sample'=8,'landmark'=16] {'landmark'}, use_global_device_ids=true, to_apply=%region_11.12 | all-reduce | flops 512 | bytes 4096 | tf_op jit(solution)/shard_map/psum | solution.py:48
  272.4 0.6 broadcast_multiply_fusion
  (1 shorter events, 0.0 us)
Async XLA Ops:
  7.2 139.1 %all-reduce.3.cloned.1.call-start = ((), (), s32[]{:S(2)}) async-start(), calls=%async_computation.1 | async-start | bytes 2097152 | tf_op jit(solution)/shard_map/psum | solution.py:40
  38.9 5.8 %copy-start = (bf16[1024,4096]{1,0:T(8,128)(2,1)S(1)}, bf16[1024,4096]{1,0:T(8,128)(2,1)}, u32[]{:S(2)}) copy-start(bf16[1024,4096]{1,0:T(8,128)(2,1)} %param.7) | copy-start | bytes 25165828
  44.7 1.7 copy-start.1
  62.6 153.8 %reduce-scatter.4.cloned.1.call-start = ((), (), s32[]{:S(2)}) async-start(), calls=%async_computation.2 | async-start | bytes 2228224
Sparse Core Ops, SparseCore 0:
  62.7 83.4 all-reduce.2
  153.8 62.5 reduce-scatter.3
